TPU v7x, 32 devices: a whole 2x2x4 slice. The times are simulated.
32 devices in a mesh: segment: 8 (over y, x, core), head: 4 (over z).
Axes of the slice: x: 2, y: 2, z: 4, core: 2. Of those that a mesh axis runs over, the one named last changes fastest.
Arguments:
- grad_in: float32 [8, 128, 512], P('segment'), may hold values from -6 to 6
- memory: bfloat16 [8, 128, 512], P('segment'), may hold values from -120 to 120
- enc_grad_in: float32 [8, 128, 512], P('segment', None, 'head'), may hold values from -3 to 3
- act_stash: bfloat16 [8, 3, 128, 512], P('segment'), may hold values from -120 to 120
- slot_order: int32 [8, 3], P('segment'), may hold values from 0 to 2, each once within a row
- lengths: int32 [8, 3], P('segment'), may hold values from 16 to 128, as said below
- w_query: bfloat16 [8, 512, 4096], P('segment', None, 'head'), may hold values from -0.0234375 to 0.0234375
- w_key: bfloat16 [8, 512, 4096], P('segment', None, 'head'), may hold values from -0.25 to 0.25
- w_value: bfloat16 [8, 512, 4096], P('segment', None, 'head'), may hold values from -0.25 to 0.25
- w_out: bfloat16 [8, 4096, 512], P('segment', 'head'), may hold values from -0.09375 to 0.09375
Outputs:
- grad_out: float32 [8, 128, 512], P('segment')
- enc_grad_out: float32 [8, 128, 512], P('segment', None, 'head')
Inputs may be any that keep to these rules, and one draw needn't show every extreme that they name: `slot_order`: each row lists every stash slot once. `lengths`: some entry equals 128.
All inputs are finite; a program needn't handle non-finite values.
Results may differ from a plain program's by a relative error of at most 0.018.
The roundings to bfloat16 on the way count: a program that leaves them out, or rounds other values in their place, can miss the bound.
Values may be sent and summed in bfloat16 or wider, within the bound.
No kernel may reach another device: no remote copies, remote signals or barrier semaphores. Data moves between devices by JAX's collectives and lax.ppermute only.
A program may use at most 64 MiB of HBM per device.

v0:
```python
import jax
import jax.numpy as jnp
from jax import lax
from jax.sharding import PartitionSpec as P

HEAD_DIM = 128
TICKS = 3


def shifted(value, axis, steps):
    count = lax.axis_size(axis)
    pairs = [(source, (source + steps) % count) for source in range(count)]
    return lax.ppermute(value, axis, pairs)


def local_terms(
    gradient_low, held, decoded, length, query_weight, key_weight, value_weight, out_weight
):
    inner = query_weight.shape[1]
    head_local = inner // HEAD_DIM
    dec_rows = decoded.shape[0]
    enc_rows = held.shape[0]
    queries = jnp.dot(decoded, query_weight, preferred_element_type=jnp.float32).astype(
        jnp.bfloat16
    )
    keys = jnp.dot(held, key_weight, preferred_element_type=jnp.float32).astype(jnp.bfloat16)
    values = jnp.dot(held, value_weight, preferred_element_type=jnp.float32).astype(jnp.bfloat16)
    query_heads = queries.reshape(dec_rows, head_local, HEAD_DIM)
    key_heads = keys.reshape(enc_rows, head_local, HEAD_DIM)
    value_heads = values.reshape(enc_rows, head_local, HEAD_DIM)
    scores = jnp.einsum("qhd,khd->hqk", query_heads, key_heads, preferred_element_type=jnp.float32)
    allowed = lax.broadcasted_iota(jnp.int32, (1, 1, enc_rows), 2) < length
    scores = jnp.where(allowed, scores, jnp.float32(-1e30))
    row_max = jnp.max(scores, axis=-1, keepdims=True)
    expo = jnp.exp(scores - row_max)
    attention = expo / jnp.sum(expo, axis=-1, keepdims=True)
    attention_low = attention.astype(jnp.bfloat16)
    context_grad = jnp.einsum(
        "qe,ie->qi", gradient_low, out_weight, preferred_element_type=jnp.float32
    ).astype(jnp.bfloat16)
    context_heads = context_grad.reshape(dec_rows, head_local, HEAD_DIM)
    prob_grad = jnp.einsum(
        "qhd,khd->hqk", context_heads, value_heads, preferred_element_type=jnp.float32
    )
    score_grad = (
        attention * (prob_grad - jnp.sum(attention * prob_grad, axis=-1, keepdims=True))
    ).astype(jnp.bfloat16)
    query_grad = (
        jnp.einsum("hqk,khd->qhd", score_grad, key_heads, preferred_element_type=jnp.float32)
        .astype(jnp.bfloat16)
        .reshape(dec_rows, inner)
    )
    key_grad = (
        jnp.einsum("hqk,qhd->khd", score_grad, query_heads, preferred_element_type=jnp.float32)
        .astype(jnp.bfloat16)
        .reshape(enc_rows, inner)
    )
    value_grad = (
        jnp.einsum("hqk,qhd->khd", attention_low, context_heads, preferred_element_type=jnp.float32)
        .astype(jnp.bfloat16)
        .reshape(enc_rows, inner)
    )
    decoder_part = jnp.einsum(
        "qi,ei->qe", query_grad, query_weight, preferred_element_type=jnp.float32
    )
    memory_part = jnp.einsum("ki,ei->ke", key_grad, key_weight, preferred_element_type=jnp.float32)
    memory_part = memory_part + jnp.einsum(
        "ki,ei->ke", value_grad, value_weight, preferred_element_type=jnp.float32
    )
    return (decoder_part, memory_part)


def body(
    grad_in, memory, enc_grad_in, act_stash, slot_order, lengths, w_query, w_key, w_value, w_out
):
    held = memory[0]
    stash_local = act_stash[0]
    order_row = slot_order[0]
    length_row = lengths[0]
    head_count = lax.axis_size("head")
    shard_width = enc_grad_in.shape[2]
    feature_share = grad_in.shape[2] // head_count
    gradient = lax.dynamic_slice_in_dim(
        grad_in[0], lax.axis_index("head") * feature_share, feature_share, 1
    )
    carried = jnp.zeros((held.shape[0], shard_width * head_count), jnp.float32)
    carried = lax.dynamic_update_slice_in_dim(
        carried, enc_grad_in[0], lax.axis_index("head") * shard_width, 1
    )
    for tick_index in range(TICKS):
        if tick_index == 0:
            gradient_low = grad_in[0].astype(jnp.bfloat16)
        else:
            gradient_low = lax.all_gather(gradient.astype(jnp.bfloat16), "head", axis=1, tiled=True)
        decoded = lax.dynamic_index_in_dim(stash_local, order_row[tick_index], 0, keepdims=False)
        decoder_part, memory_part = local_terms(
            gradient_low,
            held,
            decoded,
            length_row[tick_index],
            w_query[0],
            w_key[0],
            w_value[0],
            w_out[0],
        )
        gradient = gradient + lax.psum_scatter(
            decoder_part, "head", scatter_dimension=1, tiled=True
        )
        carried = carried + memory_part
        gradient, carried = shifted((gradient, carried), "segment", -1)
        if tick_index + 1 < TICKS:
            held = shifted(held, "segment", -1)
    carried = lax.psum_scatter(carried, "head", scatter_dimension=1, tiled=True)
    gradient = lax.all_gather(gradient, "head", axis=1, tiled=True)
    return (gradient[None], carried[None])


def solution(mesh):
    in_specs = (
        P("segment", None, None),
        P("segment", None, None),
        P("segment", None, "head"),
        P("segment", None, None, None),
        P("segment", None),
        P("segment", None),
        P("segment", None, "head"),
        P("segment", None, "head"),
        P("segment", None, "head"),
        P("segment", "head", None),
    )
    out_specs = (P("segment", None, None), P("segment", None, "head"))
    return jax.shard_map(body, mesh=mesh, in_specs=in_specs, out_specs=out_specs, check_vma=False)
```

profile of v0, /device:TPU:0, one launch (start us, length us, event | category | flops | bytes accessed | tf_op | source)
XLA Modules:
  0.0 184.4 jit_solution(5758655735363486501)
XLA Ops:
  7.2 3.4 %collective-permute-start.1 = (bf16[128,512]{1,0:T(8,128)(2,1)}, bf16[128,512]{1,0:T(8,128)(2,1)}, u32[]{:S(2)}, u32[]{:S(2)}) collective-permute-start(bf16[128,512]{1,0:T(8,128)(2,1)} %bitcast.204), channel_id=1, source_target_pairs={{0,28},{4,0},{8,4},{12,8},{16,12},{20,16},{24,20},{28,24},{1,29},{... | collective-permute-start | bytes 393224 | tf_op jit(solution)/shard_map/ppermute | solution.py:13
  12.6 1.4 fusion.66
  15.2 1.2 convolution_convert_fusion.19
  16.7 2.2 %convolution_convert_fusion.18 = bf16[128,1024]{1,0:T(8,128)(2,1)} fusion(bf16[1,1024,512]{2,1,0:T(8,128)(2,1)S(1)} %copy-done.3, f32[1,128,512]{2,1,0:T(8,128)} %param.10), kind=kOutput, calls=%fused_computation.30 | convolution fusion | flops 134414336 | bytes 1572864 | tf_op jit(solution)/shard_map/qe,ie->qi/dot_general | solution.py:38
  18.9 1.8 copy.53
  20.8 1.0 convolution_convert_fusion.20
  21.8 1.8 copy.51
  23.6 1.0 fusion.9
  24.6 2.1 %fusion.68 = (f32[8,128]{1,0:T(8,128)S(1)}, f32[8,128,128]{1,2,0:T(8,128)}) fusion(bf16[128,8,128]{0,2,1:T(8,128)(2,1)S(1)} %bitcast.191, bf16[128,8,128]{0,2,1:T(8,128)(2,1)} %bitcast.194, pred[128]{0:T(512)(128)(4,1)S(1)} %iota_compare_fusion.2), kind=kOutput, calls=%fused_computation.109 | convolution fusion | flops 33947776 | bytes 1052800 | tf_op jit(solution)/shard_map/sub | solution.py:35
  26.7 1.5 multiply_reduce_fusion.2
  28.3 0.9 copy-done.11
  29.3 1.2 fusion.28
  30.6 2.3 %convolution_convert_fusion.4 = bf16[8,128,128]{2,1,0:T(8,128)(2,1)} fusion(bf16[128,8,128]{0,2,1:T(8,128)(2,1)} %bitcast.208, f32[8,128]{1,0:T(8,128)S(1)} %get-tuple-element.8, bf16[128,8,128]{0,2,1:T(8,128)(2,1)} %bitcast.192, bf16[128,8,128]{0,2,1:T(8,128)(2,1)} %bitcast.195, pred[128]{0:T(512)(128)(4,1)S(1)} %iota_compare_fusion.2), kind=kOutput, calls=%fused_computation.16 | convolution fusion | flops 67765376 | bytes 1052800 | tf_op jit(solution)/shard_map/hqk,qhd->khd/dot_general | solution.py:59
  33.0 2.0 %convolution_convert_fusion.5 = bf16[8,128,128]{2,1,0:T(8,128)(2,1)} fusion(bf16[128,8,128]{0,2,1:T(8,128)(2,1)} %bitcast.193, bf16[8,128,128]{1,2,0:T(8,128)(2,1)S(1)} %multiply_convert_fusion.2), kind=kOutput, calls=%fused_computation.17 | convolution fusion | flops 33685504 | bytes 786432 | tf_op jit(solution)/shard_map/hqk,qhd->khd/dot_general | solution.py:54
  34.9 1.4 fusion.35
  36.4 2.2 %convolution_add_fusion.2 = f32[128,512]{1,0:T(8,128)} fusion(f32[128,512]{1,0:T(8,128)S(1)} %fusion.35, bf16[128,1024]{0,1:T(8,128)(2,1)} %bitcast.206, bf16[1,512,1024]{2,1,0:T(8,128)(2,1)S(1)} %copy-done.2), kind=kOutput, calls=%fused_computation.39 | convolution fusion | flops 134283264 | bytes 1835008 | tf_op jit(solution)/shard_map/ki,ei->ke/dot_general | solution.py:67
  38.6 1.5 fusion.60
  40.0 0.7 collective-permute-start.5
  43.9 1.9 %convolution_convert_fusion.9 = bf16[128,1024]{1,0:T(8,128)(2,1)} fusion(bf16[1,512,1024]{2,1,0:T(8,128)(2,1)S(1)} %copy-done, bf16[1,3,128,512]{3,2,1,0:T(8,128)(2,1)} %param.13, s32[]{:T(128)S(6)} %select_n.29), kind=kOutput, calls=%fused_computation.21 | convolution fusion | flops 134348800 | bytes 1441796 | tf_op jit(solution)/shard_map/dot_general | solution.py:23
  46.5 1.9 %convolution_convert_fusion.14 = bf16[128,1024]{1,0:T(8,128)(2,1)} fusion(bf16[1,512,1024]{2,1,0:T(8,128)(2,1)S(1)} %copy-done, bf16[1,3,128,512]{3,2,1,0:T(8,128)(2,1)} %param.13, s32[]{:T(128)S(6)} %select_n.27), kind=kOutput, calls=%fused_computation.26 | convolution fusion | flops 134348800 | bytes 1441796 | tf_op jit(solution)/shard_map/dot_general | solution.py:23
  49.0 1.1 copy.58
  50.2 1.9 %copy.55 = bf16[128,1024]{0,1:T(8,128)(2,1)} copy(bf16[128,1024]{1,0:T(8,128)(2,1)} %convolution_convert_fusion.14) | data formatting | bytes 524288 | tf_op jit(solution)/shard_map/reshape | solution.py:28
  52.1 0.7 iota_compare_fusion.1
  52.7 1.9 %convolution_convert_fusion.15 = bf16[128,1024]{1,0:T(8,128)(2,1)} fusion(bf16[128,512]{1,0:T(8,128)(2,1)} %collective-permute-done.1, bf16[1,512,1024]{2,1,0:T(8,128)(2,1)S(1)} %copy-done.1), kind=kOutput, calls=%fused_computation.27 | convolution fusion | flops 134348800 | bytes 1441792 | tf_op jit(solution)/shard_map/dot_general | solution.py:26
  54.7 1.8 copy.54
  56.5 2.2 %fusion.69 = (f32[8,128]{1,0:T(8,128)S(1)}, f32[8,128,128]{1,2,0:T(8,128)}) fusion(bf16[128,8,128]{0,2,1:T(8,128)(2,1)} %bitcast.185, bf16[128,8,128]{0,2,1:T(8,128)(2,1)} %bitcast.188, pred[128]{0:T(512)(128)(4,1)S(1)} %iota_compare_fusion.1), kind=kOutput, calls=%fused_computation.110 | convolution fusion | flops 33947776 | bytes 1052800 | tf_op jit(solution)/shard_map/sub | solution.py:35
  59.3 2.0 %fusion.10 = bf16[16,8,8,128]{3,2,1,0:T(8,128)(2,1)} fusion(bf16[128,512]{1,0:T(8,128)(2,1)} %collective-permute-done.1, bf16[1,512,1024]{2,1,0:T(8,128)(2,1)S(1)} %copy-done.2), kind=kOutput, calls=%fused_computation.34 | convolution fusion | flops 134348800 | bytes 1441792 | tf_op jit(solution)/shard_map/dot_general | solution.py:27
  61.2 0.9 collective-permute-done.3
  62.1 1.0 convolution_convert_fusion.10
  63.1 1.8 copy.57
  64.9 2.1 %fusion.70 = (f32[8,128]{1,0:T(8,128)S(1)}, f32[8,128,128]{1,2,0:T(8,128)}) fusion(bf16[128,8,128]{0,2,1:T(8,128)(2,1)S(1)} %bitcast.179, bf16[128,8,128]{0,2,1:T(8,128)(2,1)} %bitcast.182, pred[128]{0:T(512)(128)(4,1)S(1)} %iota_compare_fusion), kind=kOutput, calls=%fused_computation.111 | convolution fusion | flops 33947776 | bytes 1052800 | tf_op jit(solution)/shard_map/sub | solution.py:35
  67.0 1.0 bitcast_add_fusion.1
  68.0 2.7 %collective-permute-start = (f32[128,128]{1,0:T(8,128)S(1)}, f32[128,128]{1,0:T(8,128)S(1)}, u32[]{:S(2)}, u32[]{:S(2)}) collective-permute-start(f32[128,128]{1,0:T(8,128)S(1)} %bitcast_add_fusion.1), channel_id=1, source_target_pairs={{0,28},{4,0},{8,4},{12,8},{16,12},{20,16},{24,20},{28,24},{1,29},{... | collective-permute-start | bytes 196616 | tf_op jit(solution)/shard_map/ppermute | solution.py:13
  70.7 1.0 fusion.11
  71.7 0.9 collective-permute-done
  73.2 12.5 %all_gather.9 = bf16[128,512]{1,0:T(8,128)(2,1)S(1)} all-gather(bf16[128,128]{1,0:T(8,128)(2,1)S(1)} %convert_element_type.131), channel_id=1, replica_groups=mesh['segment'=8,'head'=4] {'head'}, dimensions={1}, use_global_device_ids=true | all-gather | bytes 163840 | tf_op jit(solution)/shard_map/all_gather | solution.py:94
  86.2 0.8 copy.56
  87.0 1.5 multiply_reduce_fusion.1
  88.6 0.9 copy-done.9
  89.7 1.2 fusion.25
  91.0 2.4 %convolution_convert_fusion.2 = bf16[8,128,128]{2,1,0:T(8,128)(2,1)} fusion(bf16[128,8,128]{0,2,1:T(8,128)(2,1)} %bitcast.210, f32[8,128]{1,0:T(8,128)S(1)} %get-tuple-element.12, bf16[128,8,128]{0,2,1:T(8,128)(2,1)} %bitcast.186, bf16[128,8,128]{0,2,1:T(8,128)(2,1)} %bitcast.189, pred[128]{0:T(512)(128)(4,1)S(1)} %iota_compare_fusion.1), kind=kOutput, calls=%fused_computation.14 | convolution fusion | flops 67765376 | bytes 1052800 | tf_op jit(solution)/shard_map/hqk,qhd->khd/dot_general | solution.py:59
  93.3 1.2 convolution_convert_fusion.3
  95.1 14.4 %reduce-scatter.7.cloned.1.call-done = f32[128,128]{1,0:T(8,128)} async-done(((f32[128,512]{1,0:T(8,128)}), f32[128,128]{1,0:T(8,128)}) %reduce-scatter.7.cloned.1.call-update) | async-done | bytes 65552 | tf_op jit(solution)/shard_map/reduce_scatter | solution.py:106
  109.5 0.8 add.56
  110.5 2.3 %fusion.12 = f32[128,512]{1,0:T(8,128)} fusion(f32[128,512]{1,0:T(8,128)} %collective-permute-done.5, f32[128,512]{1,0:T(8,128)S(1)} %fusion.33, bf16[128,1024]{0,1:T(8,128)(2,1)} %bitcast.213, bf16[1,512,1024]{2,1,0:T(8,128)(2,1)S(1)} %copy-done.2), kind=kOutput, calls=%fused_computation.38 | convolution fusion | flops 134348800 | bytes 2097152 | tf_op jit(solution)/shard_map/ki,ei->ke/dot_general | solution.py:67
  112.8 2.4 %collective-permute-start.6 = (f32[128,512]{1,0:T(8,128)}, f32[128,512]{1,0:T(8,128)}, u32[]{:S(2)}, u32[]{:S(2)}) collective-permute-start(f32[128,512]{1,0:T(8,128)} %fusion.12), channel_id=1, source_target_pairs={{0,28},{4,0},{8,4},{12,8},{16,12},{20,16},{24,20},{28,24},{1,29},{... | collective-permute-start | bytes 786440 | tf_op jit(solution)/shard_map/ppermute | solution.py:13
  115.2 12.3 %all_gather.10 = bf16[128,512]{1,0:T(8,128)(2,1)S(1)} all-gather(bf16[128,128]{1,0:T(8,128)(2,1)S(1)} %convert_element_type.139), channel_id=1, replica_groups=mesh['segment'=8,'head'=4] {'head'}, dimensions={1}, use_global_device_ids=true | all-gather | bytes 163840 | tf_op jit(solution)/shard_map/all_gather | solution.py:94
  127.5 1.2 convolution_convert_fusion.8
  128.7 1.8 copy.59
  130.5 2.3 %convolution_convert_fusion = bf16[8,128,128]{2,1,0:T(8,128)(2,1)} fusion(bf16[128,8,128]{0,2,1:T(8,128)(2,1)} %bitcast.211, f32[8,128]{1,0:T(8,128)S(1)} %get-tuple-element.16, bf16[128,8,128]{0,2,1:T(8,128)(2,1)S(1)} %bitcast.180, bf16[128,8,128]{0,2,1:T(8,128)(2,1)} %bitcast.183, pred[128]{0:T(512)(128)(4,1)S(1)} %iota_compare_fusion), kind=kOutput, calls=%fused_computation.12 | convolution fusion | flops 67765376 | bytes 1052800 | tf_op jit(solution)/shard_map/hqk,qhd->khd/dot_general | solution.py:59
  132.8 1.5 multiply_reduce_fusion
  134.4 1.0 convolution_convert_fusion.1
  135.6 1.2 fusion.22
  136.8 1.4 fusion.31
  138.3 0.9 copy-done.16
  139.7 1.0 add.65
  140.7 3.9 %collective-permute-done.7 = f32[128,512]{1,0:T(8,128)S(1)} collective-permute-done((f32[128,512]{1,0:T(8,128)S(1)}, f32[128,512]{1,0:T(8,128)S(1)}, u32[]{:S(2)}, u32[]{:S(2)}) %collective-permute-start.7) | collective-permute-done | bytes 262176 | tf_op jit(solution)/shard_map/ppermute | solution.py:13
  144.6 0.7 copy-done.19
  145.3 9.7 %reduce-scatter.9.cloned.1.call-done = f32[128,128]{1,0:T(8,128)} async-done(((f32[128,512]{1,0:T(8,128)}), f32[128,128]{1,0:T(8,128)}) %reduce-scatter.9.cloned.1.call-update) | async-done | bytes 65552 | tf_op jit(solution)/shard_map/reduce_scatter | solution.py:106
  155.0 0.8 add.58
  155.9 1.9 %collective-permute-done.4 = f32[128,128]{1,0:T(8,128)S(1)} collective-permute-done((f32[128,128]{1,0:T(8,128)S(1)}, f32[128,128]{1,0:T(8,128)S(1)}, u32[]{:S(2)}, u32[]{:S(2)}) %collective-permute-start.4) | collective-permute-done | bytes 65568 | tf_op jit(solution)/shard_map/ppermute | solution.py:13
  157.8 14.7 %all_gather.11 = f32[128,512]{1,0:T(8,128)S(1)} all-gather(f32[128,128]{1,0:T(8,128)S(1)} %collective-permute-done.4), channel_id=1, replica_groups=mesh['segment'=8,'head'=4] {'head'}, dimensions={1}, use_global_device_ids=true | all-gather | bytes 327680 | tf_op jit(solution)/shard_map/all_gather | solution.py:114
  172.5 4.6 %reduce-scatter.11.cloned.1.call-done = f32[128,128]{1,0:T(8,128)} async-done(((f32[128,512]{1,0:T(8,128)}), f32[128,128]{1,0:T(8,128)}) %reduce-scatter.11.cloned.1.call-update) | async-done | bytes 65552 | tf_op jit(solution)/shard_map/reduce_scatter | solution.py:113
  177.2 0.7 copy.83
  (72 shorter events, 6.1 us)
Async XLA Ops:
  7.2 8.1 %copy-start = (bf16[1,512,1024]{2,1,0:T(8,128)(2,1)S(1)}, bf16[1,512,1024]{2,1,0:T(8,128)(2,1)}, u32[]{:S(2)}) copy-start(bf16[1,512,1024]{2,1,0:T(8,128)(2,1)} %param.16) | copy-start | bytes 3145732
  7.2 3.5 %copy-start.21 = (s32[1,3]{1,0:T(1,128)S(1)}, s32[1,3]{1,0:T(1,128)}, u32[]{:S(2)}) copy-start(s32[1,3]{1,0:T(1,128)} %param.14) | copy-start | bytes 40
  7.2 9.5 %copy-start.3 = (bf16[1,1024,512]{2,1,0:T(8,128)(2,1)S(1)}, bf16[1,1024,512]{2,1,0:T(8,128)(2,1)}, u32[]{:S(2)}) copy-start(bf16[1,1024,512]{2,1,0:T(8,128)(2,1)} %param.19) | copy-start | bytes 3145732
  7.2 59.8 %reduce-scatter.5.cloned.1.call-start = ((), (), s32[]{:S(2)}) async-start(), calls=%async_computation.4 | async-start | bytes 327680 | tf_op jit(solution)/shard_map/reduce_scatter | solution.py:106
  7.2 45.5 %collective-permute-start.1 = (bf16[128,512]{1,0:T(8,128)(2,1)}, bf16[128,512]{1,0:T(8,128)(2,1)}, u32[]{:S(2)}, u32[]{:S(2)}) collective-permute-start(bf16[128,512]{1,0:T(8,128)(2,1)} %bitcast.204), channel_id=1, source_target_pairs={{0,28},{4,0},{8,4},{12,8},{16,12},{20,16},{24,20},{28,24},{1,29},{... | collective-permute-start | bytes 393224 | tf_op jit(solution)/shard_map/ppermute | solution.py:13
  16.7 7.9 %copy-start.10 = (bf16[128,1024]{0,1:T(8,128)(2,1)}, bf16[128,1024]{0,1:T(8,128)(2,1)S(1)}, u32[]{:S(2)}) copy-start(bf16[128,1024]{0,1:T(8,128)(2,1)S(1)} %copy.52) | copy-start | bytes 786436
  16.7 4.1 %copy-start.1 = (bf16[1,512,1024]{2,1,0:T(8,128)(2,1)S(1)}, bf16[1,512,1024]{2,1,0:T(8,128)(2,1)}, u32[]{:S(2)}) copy-start(bf16[1,512,1024]{2,1,0:T(8,128)(2,1)} %param.17) | copy-start | bytes 3145732
  18.9 1.8 copy-start.15
  20.7 2.8 %copy-start.2 = (bf16[1,512,1024]{2,1,0:T(8,128)(2,1)S(1)}, bf16[1,512,1024]{2,1,0:T(8,128)(2,1)}, u32[]{:S(2)}) copy-start(bf16[1,512,1024]{2,1,0:T(8,128)(2,1)} %param.18) | copy-start | bytes 3145732
  26.7 1.5 copy-start.14
  28.2 1.0 copy-start.11
  30.6 79.0 %reduce-scatter.7.cloned.1.call-start = ((), (), s32[]{:S(2)}) async-start(), calls=%async_computation.5 | async-start | bytes 327680 | tf_op jit(solution)/shard_map/reduce_scatter | solution.py:106
  36.4 2.2 %copy-start.20 = (f32[1,128,128]{2,1,0:T(8,128)S(1)}, f32[1,128,128]{2,1,0:T(8,128)}, u32[]{:S(2)}) copy-start(f32[1,128,128]{2,1,0:T(8,128)} %param.12) | copy-start | bytes 196612
  40.0 70.4 %collective-permute-start.5 = (f32[128,512]{1,0:T(8,128)}, f32[128,512]{1,0:T(8,128)}, u32[]{:S(2)}, u32[]{:S(2)}) collective-permute-start(f32[128,512]{1,0:T(8,128)} %fusion.60), channel_id=1, source_target_pairs={{0,28},{4,0},{8,4},{12,8},{16,12},{20,16},{24,20},{28,24},{1,29},{... | collective-permute-start | bytes 786440 | tf_op jit(solution)/shard_map/ppermute | solution.py:13
  50.2 14.8 %copy-start.6 = (bf16[128,1024]{0,1:T(8,128)(2,1)}, bf16[128,1024]{0,1:T(8,128)(2,1)S(1)}, u32[]{:S(2)}) copy-start(bf16[128,1024]{0,1:T(8,128)(2,1)S(1)} %copy.58) | copy-start | bytes 786436
  58.6 3.5 %collective-permute-start.3 = (bf16[128,512]{1,0:T(8,128)(2,1)}, bf16[128,512]{1,0:T(8,128)(2,1)S(1)}, u32[]{:S(2)}, u32[]{:S(2)}) collective-permute-start(bf16[128,512]{1,0:T(8,128)(2,1)} %collective-permute-done.1), channel_id=1, source_target_pairs={{0,28},{4,0},{8,4},{12,8},{16,12},{20,16},{24,20},{28,24},{1,29},{... | collective-permute-start | bytes 393224 | tf_op jit(solution)/shard_map/ppermute | solution.py:13
  67.0 18.7 %copy-start.4 = (bf16[1,1024,512]{2,1,0:T(8,128)(2,1)S(1)}, bf16[1,1024,512]{2,1,0:T(8,128)(2,1)}, u32[]{:S(2)}) copy-start(bf16[1,1024,512]{2,1,0:T(8,128)(2,1)} %param.19) | copy-start | bytes 3145732
  68.0 4.6 %collective-permute-start = (f32[128,128]{1,0:T(8,128)S(1)}, f32[128,128]{1,0:T(8,128)S(1)}, u32[]{:S(2)}, u32[]{:S(2)}) collective-permute-start(f32[128,128]{1,0:T(8,128)S(1)} %bitcast_add_fusion.1), channel_id=1, source_target_pairs={{0,28},{4,0},{8,4},{12,8},{16,12},{20,16},{24,20},{28,24},{1,29},{... | collective-permute-start | bytes 196616 | tf_op jit(solution)/shard_map/ppermute | solution.py:13
  72.6 0.6 copy-start.17
  87.0 1.5 copy-start.13
  88.5 1.0 copy-start.9
  90.9 64.1 %reduce-scatter.9.cloned.1.call-start = ((), (), s32[]{:S(2)}) async-start(), calls=%async_computation.6 | async-start | bytes 327680 | tf_op jit(solution)/shard_map/reduce_scatter | solution.py:106
  94.6 14.9 %copy-start.18 = (f32[128,128]{1,0:T(8,128)S(1)}, f32[128,128]{1,0:T(8,128)}, u32[]{:S(2)}) copy-start(f32[128,128]{1,0:T(8,128)} %copy-done.17) | copy-start | bytes 196612
  110.4 4.8 %collective-permute-start.2 = (f32[128,128]{1,0:T(8,128)S(1)}, f32[128,128]{1,0:T(8,128)S(1)}, u32[]{:S(2)}, u32[]{:S(2)}) collective-permute-start(f32[128,128]{1,0:T(8,128)S(1)} %add.56), channel_id=1, source_target_pairs={{0,28},{4,0},{8,4},{12,8},{16,12},{20,16},{24,20},{28,24},{1,29},{... | collective-permute-start | bytes 196616 | tf_op jit(solution)/shard_map/ppermute | solution.py:13
  110.5 17.0 %copy-start.5 = (bf16[1,1024,512]{2,1,0:T(8,128)(2,1)S(1)}, bf16[1,1024,512]{2,1,0:T(8,128)(2,1)}, u32[]{:S(2)}) copy-start(bf16[1,1024,512]{2,1,0:T(8,128)(2,1)} %param.19) | copy-start | bytes 3145732
  112.8 26.9 %collective-permute-start.6 = (f32[128,512]{1,0:T(8,128)}, f32[128,512]{1,0:T(8,128)}, u32[]{:S(2)}, u32[]{:S(2)}) collective-permute-start(f32[128,512]{1,0:T(8,128)} %fusion.12), channel_id=1, source_target_pairs={{0,28},{4,0},{8,4},{12,8},{16,12},{20,16},{24,20},{28,24},{1,29},{... | collective-permute-start | bytes 786440 | tf_op jit(solution)/shard_map/ppermute | solution.py:13
  128.7 1.8 copy-start.7
  132.8 1.5 copy-start.12
  134.4 1.0 copy-start.8
  138.2 1.0 copy-start.16
  138.3 38.9 %reduce-scatter.11.cloned.1.call-start = ((), (), s32[]{:S(2)}) async-start(), calls=%async_computation.7 | async-start | bytes 327680 | tf_op jit(solution)/shard_map/reduce_scatter | solution.py:113
  140.7 3.9 %collective-permute-start.7 = (f32[128,512]{1,0:T(8,128)S(1)}, f32[128,512]{1,0:T(8,128)S(1)}, u32[]{:S(2)}, u32[]{:S(2)}) collective-permute-start(f32[128,512]{1,0:T(8,128)S(1)} %add.65), channel_id=1, source_target_pairs={{0,28},{4,0},{8,4},{12,8},{16,12},{20,16},{24,20},{28,24},{1,29},{... | collective-permute-start | bytes 786440 | tf_op jit(solution)/shard_map/ppermute | solution.py:13
  144.6 0.7 copy-start.19
  155.9 2.0 %collective-permute-start.4 = (f32[128,128]{1,0:T(8,128)S(1)}, f32[128,128]{1,0:T(8,128)S(1)}, u32[]{:S(2)}, u32[]{:S(2)}) collective-permute-start(f32[128,128]{1,0:T(8,128)S(1)} %add.58), channel_id=1, source_target_pairs={{0,28},{4,0},{8,4},{12,8},{16,12},{20,16},{24,20},{28,24},{1,29},{... | collective-permute-start | bytes 196616 | tf_op jit(solution)/shard_map/ppermute | solution.py:13
Sparse Core Ops, SparseCore 0:
  30.7 19.9 reduce-scatter.4
  91.1 18.4 reduce-scatter.6
  138.4 16.6 reduce-scatter.8
  157.7 19.3 reduce-scatter.10
where the time goes:
time: 186 us; the launch traced here: 184 us
  matrix products  51.4 us (28%)
  blocking collectives  39.4 us (21%)
  waiting for transfers between devices  36.4 us (20%)
  between operations  19.9 us (11%)
  local copies, waits for them, and re-layouts  19.8 us (11%)
  starting transfers between devices  10.2 us (5%)
  other arithmetic  7.23 us (4%)
    all_gather x2, blocking collectives, body(): lax.all_gather(gradient.astype(jnp.bfloat16), 'head', axis=1, tiled=True)  24.7 us
    reduce_scatter x3, waiting for transfers between devices, body(): lax.psum_scatter(decoder_part, 'head', scatter_dimension=1, tiled=True)  24.2 us
    all_gather x1, blocking collectives, body(): gradient = lax.all_gather(gradient, 'head', axis=1, tiled=True)  14.7 us
    ppermute x8, starting transfers between devices, shifted(): return lax.ppermute(value, axis, pairs)  10 us
    ppermute x8, waiting for transfers between devices, shifted(): return lax.ppermute(value, axis, pairs)  7.54 us
    dot_general x3, matrix products, local_terms(): jnp.einsum('hqk,qhd->khd', attention_low, context_heads, preferred_elemen...  6.98 us
    sub x3, matrix products, local_terms(): expo = jnp.exp(scores - row_max)  6.36 us
    reshape x3, local copies, waits for them, and re-layouts, local_terms(): key_heads = keys.reshape(enc_rows, head_local, HEAD_DIM)  5.37 us
  transfers between devices with their start and end apart: 12, of which 7 were waited for; matrix products, arithmetic and copies ran while one was open for 40% of the time, Pallas kernels for 0%

commit v1 on v0

--- a/solution.py
+++ b/solution.py
@@ -111,7 +111,12 @@
         if tick_index + 1 < TICKS:
             held = shifted(held, "segment", -1)
     carried = lax.psum_scatter(carried, "head", scatter_dimension=1, tiled=True)
-    gradient = lax.all_gather(gradient, "head", axis=1, tiled=True)
+    ring = [gradient]
+    for hop in range(3):
+        ring.append(lax.ppermute(ring[-1], "head", [(dev, (dev + 1) % 4) for dev in range(4)]))
+    gradient = jnp.roll(
+        jnp.concatenate(ring[::-1], axis=1), (lax.axis_index("head") + 1) * ring[0].shape[1], axis=1
+    )
     return (gradient[None], carried[None])
 
 

time: 186 us -> 199 us (1.070)
  waiting for transfers between devices: 36.4 us -> 62.4 us
  blocking collectives: 39.4 us -> 24.7 us
  starting transfers between devices: 10.2 us -> 12.7 us
    ppermute x0 -> x3, waiting for transfers between devices: none -> 17.5 us  [body(): lax.ppermute(ring[-1], 'head', [(dev, (dev + 1) % 4) for dev in range(4)])]
    all_gather x1 -> x0, blocking collectives: 14.7 us -> none  [body(): gradient = lax.all_gather(gradient, 'head', axis=1, tiled=True)]
    reduce_scatter x1, waiting for transfers between devices: 4.63 us -> 14.2 us  [body(): carried = lax.psum_scatter(carried, 'head', scatter_dimension=1, tiled=True)]
    ppermute x8, waiting for transfers between devices: 7.54 us -> 1.8 us  [shifted(): return lax.ppermute(value, axis, pairs)]
    reduce_scatter x3, waiting for transfers between devices: 24.2 us -> 28.8 us  [body(): lax.psum_scatter(decoder_part, 'head', scatter_dimension=1, tiled=True)]
    ppermute x8, starting transfers between devices: 10 us -> 12.5 us  [shifted(): return lax.ppermute(value, axis, pairs)]
    unnamed x45 -> x53, local copies, waits for them, and re-layouts: 4.67 us -> 4.5 us
  transfers between devices with their start and end apart: 12 -> 15, of which waited for: 7 -> 8; matrix products, arithmetic and copies ran while one was open for 40% -> 37% of each run, Pallas kernels for 0% -> 0%
where the time goes in v1:
time: 199 us; the launch traced here: 198 us
  waiting for transfers between devices  62.4 us (31%)
  matrix products  50.5 us (25%)
  blocking collectives  24.7 us (12%)
  local copies, waits for them, and re-layouts  20.4 us (10%)
  between operations  20 us (10%)
  starting transfers between devices  12.7 us (6%)
  other arithmetic  7.28 us (4%)
    reduce_scatter x3, waiting for transfers between devices, body(): lax.psum_scatter(decoder_part, 'head', scatter_dimension=1, tiled=True)  28.8 us
    all_gather x2, blocking collectives, body(): lax.all_gather(gradient.astype(jnp.bfloat16), 'head', axis=1, tiled=True)  24.7 us
    ppermute x3, waiting for transfers between devices, body(): lax.ppermute(ring[-1], 'head', [(dev, (dev + 1) % 4) for dev in range(4)])  17.5 us
    reduce_scatter x1, waiting for transfers between devices, body(): carried = lax.psum_scatter(carried, 'head', scatter_dimension=1, tiled=True)  14.2 us
    ppermute x8, starting transfers between devices, shifted(): return lax.ppermute(value, axis, pairs)  12.5 us
    dot_general x3, matrix products, local_terms(): jnp.einsum('hqk,qhd->khd', attention_low, context_heads, preferred_elemen...  7.01 us
    sub x3, matrix products, local_terms(): expo = jnp.exp(scores - row_max)  6.36 us
    reshape x3, local copies, waits for them, and re-layouts, local_terms(): key_heads = keys.reshape(enc_rows, head_local, HEAD_DIM)  5.36 us
  transfers between devices with their start and end apart: 15, of which 8 were waited for; matrix products, arithmetic and copies ran while one was open for 37% of the time, Pallas kernels for 0%

profile of v1, /device:TPU:0, one launch (start us, length us, event | category | flops | bytes accessed | tf_op | source)
XLA Modules:
  0.0 197.9 jit_solution(13779317488252456091)
XLA Ops:
  7.2 3.4 %collective-permute-start.1 = (bf16[128,512]{1,0:T(8,128)(2,1)}, bf16[128,512]{1,0:T(8,128)(2,1)}, u32[]{:S(2)}, u32[]{:S(2)}) collective-permute-start(bf16[128,512]{1,0:T(8,128)(2,1)} %bitcast.204), channel_id=1, source_target_pairs={{0,28},{4,0},{8,4},{12,8},{16,12},{20,16},{24,20},{28,24},{1,29},{... | collective-permute-start | bytes 393224 | tf_op jit(solution)/shard_map/ppermute | solution.py:13
  10.7 0.6 fusion.67
  12.6 1.4 fusion.66
  15.3 1.2 convolution_convert_fusion.19
  16.8 2.2 %convolution_convert_fusion.18 = bf16[128,1024]{1,0:T(8,128)(2,1)} fusion(bf16[1,1024,512]{2,1,0:T(8,128)(2,1)S(1)} %copy-done.3, f32[1,128,512]{2,1,0:T(8,128)} %param.10), kind=kOutput, calls=%fused_computation.30 | convolution fusion | flops 134414336 | bytes 1572864 | tf_op jit(solution)/shard_map/qe,ie->qi/dot_general | solution.py:38
  19.0 1.8 copy.53
  20.8 1.0 convolution_convert_fusion.20
  21.9 1.8 copy.51
  23.7 1.0 fusion.9
  24.7 2.1 %fusion.68 = (f32[8,128]{1,0:T(8,128)S(1)}, f32[8,128,128]{1,2,0:T(8,128)}) fusion(bf16[128,8,128]{0,2,1:T(8,128)(2,1)S(1)} %bitcast.192, bf16[128,8,128]{0,2,1:T(8,128)(2,1)} %bitcast.195, pred[128]{0:T(512)(128)(4,1)S(1)} %iota_compare_fusion.2), kind=kOutput, calls=%fused_computation.118 | convolution fusion | flops 33947776 | bytes 1052800 | tf_op jit(solution)/shard_map/sub | solution.py:35
  26.8 1.5 multiply_reduce_fusion.2
  28.4 0.9 copy-done.11
  29.4 1.2 fusion.28
  30.7 2.4 %convolution_convert_fusion.4 = bf16[8,128,128]{2,1,0:T(8,128)(2,1)} fusion(bf16[128,8,128]{0,2,1:T(8,128)(2,1)} %bitcast.208, f32[8,128]{1,0:T(8,128)S(1)} %get-tuple-element.8, bf16[128,8,128]{0,2,1:T(8,128)(2,1)} %bitcast.193, bf16[128,8,128]{0,2,1:T(8,128)(2,1)} %bitcast.196, pred[128]{0:T(512)(128)(4,1)S(1)} %iota_compare_fusion.2), kind=kOutput, calls=%fused_computation.16 | convolution fusion | flops 67765376 | bytes 1052800 | tf_op jit(solution)/shard_map/hqk,qhd->khd/dot_general | solution.py:59
  33.1 1.9 convolution_convert_fusion.5
  35.0 1.4 fusion.35
  36.5 2.2 %convolution_add_fusion.2 = f32[128,512]{1,0:T(8,128)} fusion(f32[128,512]{1,0:T(8,128)S(1)} %fusion.35, bf16[128,1024]{0,1:T(8,128)(2,1)} %bitcast.206, bf16[1,512,1024]{2,1,0:T(8,128)(2,1)S(1)} %copy-done.2), kind=kOutput, calls=%fused_computation.39 | convolution fusion | flops 134283264 | bytes 1835008 | tf_op jit(solution)/shard_map/ki,ei->ke/dot_general | solution.py:67
  38.7 1.5 fusion.60
  40.2 0.7 collective-permute-start.8
  44.0 1.9 convolution_convert_fusion.9
  46.6 1.9 convolution_convert_fusion.14
  49.2 1.1 copy.58
  50.3 1.9 copy.55
  52.8 1.9 convolution_convert_fusion.15
  54.7 1.8 copy.54
  56.5 2.2 %fusion.69 = (f32[8,128]{1,0:T(8,128)S(1)}, f32[8,128,128]{1,2,0:T(8,128)}) fusion(bf16[128,8,128]{0,2,1:T(8,128)(2,1)} %bitcast.186, bf16[128,8,128]{0,2,1:T(8,128)(2,1)} %bitcast.189, pred[128]{0:T(512)(128)(4,1)S(1)} %iota_compare_fusion.1), kind=kOutput, calls=%fused_computation.119 | convolution fusion | flops 33947776 | bytes 1052800 | tf_op jit(solution)/shard_map/sub | solution.py:35
  59.3 1.9 fusion.10
  61.3 0.9 collective-permute-done.3
  62.2 1.0 convolution_convert_fusion.10
  63.2 1.8 copy.57
  64.9 2.1 %fusion.70 = (f32[8,128]{1,0:T(8,128)S(1)}, f32[8,128,128]{1,2,0:T(8,128)}) fusion(bf16[128,8,128]{0,2,1:T(8,128)(2,1)S(1)} %bitcast.180, bf16[128,8,128]{0,2,1:T(8,128)(2,1)} %bitcast.183, pred[128]{0:T(512)(128)(4,1)S(1)} %iota_compare_fusion), kind=kOutput, calls=%fused_computation.120 | convolution fusion | flops 33947776 | bytes 1052800 | tf_op jit(solution)/shard_map/sub | solution.py:35
  67.0 1.0 bitcast_add_fusion.1
  68.0 2.7 %collective-permute-start = (f32[128,128]{1,0:T(8,128)S(1)}, f32[128,128]{1,0:T(8,128)S(1)}, u32[]{:S(2)}, u32[]{:S(2)}) collective-permute-start(f32[128,128]{1,0:T(8,128)S(1)} %bitcast_add_fusion.1), channel_id=1, source_target_pairs={{0,28},{4,0},{8,4},{12,8},{16,12},{20,16},{24,20},{28,24},{1,29},{... | collective-permute-start | bytes 196616 | tf_op jit(solution)/shard_map/ppermute | solution.py:13
  70.7 1.0 fusion.11
  71.7 0.9 collective-permute-done
  73.3 12.5 %all_gather.6 = bf16[128,512]{1,0:T(8,128)(2,1)S(1)} all-gather(bf16[128,128]{1,0:T(8,128)(2,1)S(1)} %convert_element_type.131), channel_id=1, replica_groups=mesh['segment'=8,'head'=4] {'head'}, dimensions={1}, use_global_device_ids=true | all-gather | bytes 163840 | tf_op jit(solution)/shard_map/all_gather | solution.py:94
  86.2 0.8 copy.56
  87.1 1.5 multiply_reduce_fusion.1
  88.6 0.9 copy-done.9
  89.7 1.2 fusion.25
  91.0 2.4 %convolution_convert_fusion.2 = bf16[8,128,128]{2,1,0:T(8,128)(2,1)} fusion(bf16[128,8,128]{0,2,1:T(8,128)(2,1)} %bitcast.210, f32[8,128]{1,0:T(8,128)S(1)} %get-tuple-element.12, bf16[128,8,128]{0,2,1:T(8,128)(2,1)} %bitcast.187, bf16[128,8,128]{0,2,1:T(8,128)(2,1)} %bitcast.190, pred[128]{0:T(512)(128)(4,1)S(1)} %iota_compare_fusion.1), kind=kOutput, calls=%fused_computation.14 | convolution fusion | flops 67765376 | bytes 1052800 | tf_op jit(solution)/shard_map/hqk,qhd->khd/dot_general | solution.py:59
  93.4 1.2 convolution_convert_fusion.3
  95.1 14.4 %reduce-scatter.7.cloned.1.call-done = f32[128,128]{1,0:T(8,128)} async-done(((f32[128,512]{1,0:T(8,128)}), f32[128,128]{1,0:T(8,128)}) %reduce-scatter.7.cloned.1.call-update) | async-done | bytes 65552 | tf_op jit(solution)/shard_map/reduce_scatter | solution.py:106
  109.5 0.8 add.69
  110.4 2.3 %fusion.12 = f32[128,512]{1,0:T(8,128)} fusion(f32[128,512]{1,0:T(8,128)} %collective-permute-done.8, f32[128,512]{1,0:T(8,128)S(1)} %fusion.33, bf16[128,1024]{0,1:T(8,128)(2,1)} %bitcast.213, bf16[1,512,1024]{2,1,0:T(8,128)(2,1)S(1)} %copy-done.2), kind=kOutput, calls=%fused_computation.38 | convolution fusion | flops 134348800 | bytes 2097152 | tf_op jit(solution)/shard_map/ki,ei->ke/dot_general | solution.py:67
  112.8 2.5 %collective-permute-start.9 = (f32[128,512]{1,0:T(8,128)}, f32[128,512]{1,0:T(8,128)}, u32[]{:S(2)}, u32[]{:S(2)}) collective-permute-start(f32[128,512]{1,0:T(8,128)} %fusion.12), channel_id=1, source_target_pairs={{0,28},{4,0},{8,4},{12,8},{16,12},{20,16},{24,20},{28,24},{1,29},{... | collective-permute-start | bytes 786440 | tf_op jit(solution)/shard_map/ppermute | solution.py:13
  115.2 12.3 %all_gather.7 = bf16[128,512]{1,0:T(8,128)(2,1)S(1)} all-gather(bf16[128,128]{1,0:T(8,128)(2,1)S(1)} %convert_element_type.139), channel_id=1, replica_groups=mesh['segment'=8,'head'=4] {'head'}, dimensions={1}, use_global_device_ids=true | all-gather | bytes 163840 | tf_op jit(solution)/shard_map/all_gather | solution.py:94
  127.5 1.2 convolution_convert_fusion.8
  128.7 1.8 copy.59
  130.5 2.3 %convolution_convert_fusion = bf16[8,128,128]{2,1,0:T(8,128)(2,1)} fusion(bf16[128,8,128]{0,2,1:T(8,128)(2,1)} %bitcast.211, f32[8,128]{1,0:T(8,128)S(1)} %get-tuple-element.16, bf16[128,8,128]{0,2,1:T(8,128)(2,1)S(1)} %bitcast.181, bf16[128,8,128]{0,2,1:T(8,128)(2,1)} %bitcast.184, pred[128]{0:T(512)(128)(4,1)S(1)} %iota_compare_fusion), kind=kOutput, calls=%fused_computation.12 | convolution fusion | flops 67765376 | bytes 1052800 | tf_op jit(solution)/shard_map/hqk,qhd->khd/dot_general | solution.py:59
  132.8 1.5 multiply_reduce_fusion
  134.4 1.0 convolution_convert_fusion.1
  135.6 1.2 fusion.22
  136.9 0.9 copy-done.12
  139.2 14.4 %reduce-scatter.9.cloned.1.call-done = f32[128,128]{1,0:T(8,128)} async-done(((f32[128,512]{1,0:T(8,128)}), f32[128,128]{1,0:T(8,128)}) %reduce-scatter.9.cloned.1.call-update) | async-done | bytes 65552 | tf_op jit(solution)/shard_map/reduce_scatter | solution.py:106
  153.7 0.8 add.71
  154.6 1.0 add.81
  155.6 2.5 %collective-permute-start.10 = (f32[128,512]{1,0:T(8,128)S(1)}, f32[128,512]{1,0:T(8,128)S(1)}, u32[]{:S(2)}, u32[]{:S(2)}) collective-permute-start(f32[128,512]{1,0:T(8,128)S(1)} %add.81), channel_id=1, source_target_pairs={{0,28},{4,0},{8,4},{12,8},{16,12},{20,16},{24,20},{28,24},{1,29},{... | collective-permute-start | bytes 786440 | tf_op jit(solution)/shard_map/ppermute | solution.py:13
  158.1 6.1 %collective-permute-done.5 = f32[128,128]{1,0:T(8,128)S(1)} collective-permute-done((f32[128,128]{1,0:T(8,128)S(1)}, f32[128,128]{1,0:T(8,128)S(1)}, u32[]{:S(2)}, u32[]{:S(2)}) %collective-permute-start.5) | collective-permute-done | bytes 65568 | tf_op jit(solution)/shard_map/ppermute | solution.py:116
  164.1 6.1 %collective-permute-done.6 = f32[128,128]{1,0:T(8,128)S(1)} collective-permute-done((f32[128,128]{1,0:T(8,128)S(1)}, f32[128,128]{1,0:T(8,128)S(1)}, u32[]{:S(2)}, u32[]{:S(2)}) %collective-permute-start.6) | collective-permute-done | bytes 65568 | tf_op jit(solution)/shard_map/ppermute | solution.py:116
  170.2 0.7 copy-done.20
  170.9 5.3 %collective-permute-done.7 = f32[128,128]{1,0:T(8,128)S(1)} collective-permute-done((f32[128,128]{1,0:T(8,128)S(1)}, f32[128,128]{1,0:T(8,128)S(1)}, u32[]{:S(2)}, u32[]{:S(2)}) %collective-permute-start.7) | collective-permute-done | bytes 65568 | tf_op jit(solution)/shard_map/ppermute | solution.py:116
  176.4 0.7 dynamic-slice_bitcast_fusion
  177.1 14.2 %reduce-scatter.11.cloned.1.call-done = f32[128,128]{1,0:T(8,128)} async-done(((f32[128,512]{1,0:T(8,128)}), f32[128,128]{1,0:T(8,128)}) %reduce-scatter.11.cloned.1.call-update) | async-done | bytes 65552 | tf_op jit(solution)/shard_map/reduce_scatter | solution.py:113
  (87 shorter events, 7.1 us)
Async XLA Ops:
  7.2 8.2 %copy-start = (bf16[1,512,1024]{2,1,0:T(8,128)(2,1)S(1)}, bf16[1,512,1024]{2,1,0:T(8,128)(2,1)}, u32[]{:S(2)}) copy-start(bf16[1,512,1024]{2,1,0:T(8,128)(2,1)} %param.16) | copy-start | bytes 3145732
  7.2 3.5 %copy-start.22 = (s32[1,3]{1,0:T(1,128)S(1)}, s32[1,3]{1,0:T(1,128)}, u32[]{:S(2)}) copy-start(s32[1,3]{1,0:T(1,128)} %param.14) | copy-start | bytes 40
  7.2 9.5 %copy-start.3 = (bf16[1,1024,512]{2,1,0:T(8,128)(2,1)S(1)}, bf16[1,1024,512]{2,1,0:T(8,128)(2,1)}, u32[]{:S(2)}) copy-start(bf16[1,1024,512]{2,1,0:T(8,128)(2,1)} %param.19) | copy-start | bytes 3145732
  7.2 59.8 %reduce-scatter.5.cloned.1.call-start = ((), (), s32[]{:S(2)}) async-start(), calls=%async_computation.4 | async-start | bytes 327680 | tf_op jit(solution)/shard_map/reduce_scatter | solution.py:106
  7.2 45.6 %collective-permute-start.1 = (bf16[128,512]{1,0:T(8,128)(2,1)}, bf16[128,512]{1,0:T(8,128)(2,1)}, u32[]{:S(2)}, u32[]{:S(2)}) collective-permute-start(bf16[128,512]{1,0:T(8,128)(2,1)} %bitcast.204), channel_id=1, source_target_pairs={{0,28},{4,0},{8,4},{12,8},{16,12},{20,16},{24,20},{28,24},{1,29},{... | collective-permute-start | bytes 393224 | tf_op jit(solution)/shard_map/ppermute | solution.py:13
  16.7 7.9 %copy-start.10 = (bf16[128,1024]{0,1:T(8,128)(2,1)}, bf16[128,1024]{0,1:T(8,128)(2,1)S(1)}, u32[]{:S(2)}) copy-start(bf16[128,1024]{0,1:T(8,128)(2,1)S(1)} %copy.52) | copy-start | bytes 786436
  16.8 4.1 %copy-start.1 = (bf16[1,512,1024]{2,1,0:T(8,128)(2,1)S(1)}, bf16[1,512,1024]{2,1,0:T(8,128)(2,1)}, u32[]{:S(2)}) copy-start(bf16[1,512,1024]{2,1,0:T(8,128)(2,1)} %param.17) | copy-start | bytes 3145732
  19.0 1.8 copy-start.16
  20.8 2.8 %copy-start.2 = (bf16[1,512,1024]{2,1,0:T(8,128)(2,1)S(1)}, bf16[1,512,1024]{2,1,0:T(8,128)(2,1)}, u32[]{:S(2)}) copy-start(bf16[1,512,1024]{2,1,0:T(8,128)(2,1)} %param.18) | copy-start | bytes 3145732
  26.8 1.5 copy-start.15
  28.3 1.0 copy-start.11
  30.7 78.9 %reduce-scatter.7.cloned.1.call-start = ((), (), s32[]{:S(2)}) async-start(), calls=%async_computation.5 | async-start | bytes 327680 | tf_op jit(solution)/shard_map/reduce_scatter | solution.py:106
  36.5 2.2 %copy-start.21 = (f32[1,128,128]{2,1,0:T(8,128)S(1)}, f32[1,128,128]{2,1,0:T(8,128)}, u32[]{:S(2)}) copy-start(f32[1,128,128]{2,1,0:T(8,128)} %param.12) | copy-start | bytes 196612
  40.2 70.3 %collective-permute-start.8 = (f32[128,512]{1,0:T(8,128)}, f32[128,512]{1,0:T(8,128)}, u32[]{:S(2)}, u32[]{:S(2)}) collective-permute-start(f32[128,512]{1,0:T(8,128)} %fusion.60), channel_id=1, source_target_pairs={{0,28},{4,0},{8,4},{12,8},{16,12},{20,16},{24,20},{28,24},{1,29},{... | collective-permute-start | bytes 786440 | tf_op jit(solution)/shard_map/ppermute | solution.py:13
  50.3 14.7 %copy-start.6 = (bf16[128,1024]{0,1:T(8,128)(2,1)}, bf16[128,1024]{0,1:T(8,128)(2,1)S(1)}, u32[]{:S(2)}) copy-start(bf16[128,1024]{0,1:T(8,128)(2,1)S(1)} %copy.58) | copy-start | bytes 786436
  58.7 3.5 %collective-permute-start.3 = (bf16[128,512]{1,0:T(8,128)(2,1)}, bf16[128,512]{1,0:T(8,128)(2,1)S(1)}, u32[]{:S(2)}, u32[]{:S(2)}) collective-permute-start(bf16[128,512]{1,0:T(8,128)(2,1)} %collective-permute-done.1), channel_id=1, source_target_pairs={{0,28},{4,0},{8,4},{12,8},{16,12},{20,16},{24,20},{28,24},{1,29},{... | collective-permute-start | bytes 393224 | tf_op jit(solution)/shard_map/ppermute | solution.py:13
  67.0 18.7 %copy-start.4 = (bf16[1,1024,512]{2,1,0:T(8,128)(2,1)S(1)}, bf16[1,1024,512]{2,1,0:T(8,128)(2,1)}, u32[]{:S(2)}) copy-start(bf16[1,1024,512]{2,1,0:T(8,128)(2,1)} %param.19) | copy-start | bytes 3145732
  68.0 4.6 %collective-permute-start = (f32[128,128]{1,0:T(8,128)S(1)}, f32[128,128]{1,0:T(8,128)S(1)}, u32[]{:S(2)}, u32[]{:S(2)}) collective-permute-start(f32[128,128]{1,0:T(8,128)S(1)} %bitcast_add_fusion.1), channel_id=1, source_target_pairs={{0,28},{4,0},{8,4},{12,8},{16,12},{20,16},{24,20},{28,24},{1,29},{... | collective-permute-start | bytes 196616 | tf_op jit(solution)/shard_map/ppermute | solution.py:13
  72.6 0.6 copy-start.18
  87.0 1.5 copy-start.14
  88.6 1.0 copy-start.9
  90.9 62.7 %reduce-scatter.9.cloned.1.call-start = ((), (), s32[]{:S(2)}) async-start(), calls=%async_computation.6 | async-start | bytes 327680 | tf_op jit(solution)/shard_map/reduce_scatter | solution.py:106
  94.6 14.9 %copy-start.19 = (f32[128,128]{1,0:T(8,128)S(1)}, f32[128,128]{1,0:T(8,128)}, u32[]{:S(2)}) copy-start(f32[128,128]{1,0:T(8,128)} %copy-done.18) | copy-start | bytes 196612
  110.4 4.9 %collective-permute-start.2 = (f32[128,128]{1,0:T(8,128)S(1)}, f32[128,128]{1,0:T(8,128)S(1)}, u32[]{:S(2)}, u32[]{:S(2)}) collective-permute-start(f32[128,128]{1,0:T(8,128)S(1)} %add.69), channel_id=1, source_target_pairs={{0,28},{4,0},{8,4},{12,8},{16,12},{20,16},{24,20},{28,24},{1,29},{... | collective-permute-start | bytes 196616 | tf_op jit(solution)/shard_map/ppermute | solution.py:13
  110.4 17.1 %copy-start.5 = (bf16[1,1024,512]{2,1,0:T(8,128)(2,1)S(1)}, bf16[1,1024,512]{2,1,0:T(8,128)(2,1)}, u32[]{:S(2)}) copy-start(bf16[1,1024,512]{2,1,0:T(8,128)(2,1)} %param.19) | copy-start | bytes 3145732
  112.8 41.8 %collective-permute-start.9 = (f32[128,512]{1,0:T(8,128)}, f32[128,512]{1,0:T(8,128)}, u32[]{:S(2)}, u32[]{:S(2)}) collective-permute-start(f32[128,512]{1,0:T(8,128)} %fusion.12), channel_id=1, source_target_pairs={{0,28},{4,0},{8,4},{12,8},{16,12},{20,16},{24,20},{28,24},{1,29},{... | collective-permute-start | bytes 786440 | tf_op jit(solution)/shard_map/ppermute | solution.py:13
  128.7 1.8 copy-start.7
  132.8 1.5 copy-start.13
  134.4 1.0 copy-start.8
  136.8 0.9 copy-start.12
  136.9 54.5 %reduce-scatter.11.cloned.1.call-start = ((), (), s32[]{:S(2)}) async-start(), calls=%async_computation.7 | async-start | bytes 327680 | tf_op jit(solution)/shard_map/reduce_scatter | solution.py:113
  137.8 0.9 copy-start.17
  154.5 3.6 %collective-permute-start.4 = (f32[128,128]{1,0:T(8,128)S(1)}, f32[128,128]{1,0:T(8,128)S(1)}, u32[]{:S(2)}, u32[]{:S(2)}) collective-permute-start(f32[128,128]{1,0:T(8,128)S(1)} %add.71), channel_id=1, source_target_pairs={{0,28},{4,0},{8,4},{12,8},{16,12},{20,16},{24,20},{28,24},{1,29},{... | collective-permute-start | bytes 196616 | tf_op jit(solution)/shard_map/ppermute | solution.py:13
  155.6 14.6 %collective-permute-start.10 = (f32[128,512]{1,0:T(8,128)S(1)}, f32[128,512]{1,0:T(8,128)S(1)}, u32[]{:S(2)}, u32[]{:S(2)}) collective-permute-start(f32[128,512]{1,0:T(8,128)S(1)} %add.81), channel_id=1, source_target_pairs={{0,28},{4,0},{8,4},{12,8},{16,12},{20,16},{24,20},{28,24},{1,29},{... | collective-permute-start | bytes 786440 | tf_op jit(solution)/shard_map/ppermute | solution.py:13
  158.1 6.1 %collective-permute-start.5 = (f32[128,128]{1,0:T(8,128)S(1)}, f32[128,128]{1,0:T(8,128)S(1)}, u32[]{:S(2)}, u32[]{:S(2)}) collective-permute-start(f32[128,128]{1,0:T(8,128)S(1)} %collective-permute-done.4), channel_id=1, source_target_pairs={{0,1},{1,2},{2,3},{3,0},{4,5},{5,6},{6,7},{7,4},{8,9},{9,10},{10,1... | collective-permute-start | bytes 196616 | tf_op jit(solution)/shard_map/ppermute | solution.py:116
  164.1 6.1 %collective-permute-start.6 = (f32[128,128]{1,0:T(8,128)S(1)}, f32[128,128]{1,0:T(8,128)S(1)}, u32[]{:S(2)}, u32[]{:S(2)}) collective-permute-start(f32[128,128]{1,0:T(8,128)S(1)} %collective-permute-done.5), channel_id=1, source_target_pairs={{0,1},{1,2},{2,3},{3,0},{4,5},{5,6},{6,7},{7,4},{8,9},{9,10},{10,1... | collective-permute-start | bytes 196616 | tf_op jit(solution)/shard_map/ppermute | solution.py:116
  170.2 6.1 %collective-permute-start.7 = (f32[128,128]{1,0:T(8,128)S(1)}, f32[128,128]{1,0:T(8,128)S(1)}, u32[]{:S(2)}, u32[]{:S(2)}) collective-permute-start(f32[128,128]{1,0:T(8,128)S(1)} %collective-permute-done.6), channel_id=1, source_target_pairs={{0,1},{1,2},{2,3},{3,0},{4,5},{5,6},{6,7},{7,4},{8,9},{9,10},{10,1... | collective-permute-start | bytes 196616 | tf_op jit(solution)/shard_map/ppermute | solution.py:116
  170.2 0.7 copy-start.20
Sparse Core Ops, SparseCore 0:
  30.8 19.9 reduce-scatter.4
  91.1 18.4 reduce-scatter.6
  137.0 16.6 reduce-scatter.8
  171.1 20.2 reduce-scatter.10
